TPU v7x, 32 devices: a whole 2x2x4 slice. The times are simulated.
32 devices in a mesh: rep: 4 (over z), shard: 8 (over y, x, core).
Axes of the slice: x: 2, y: 2, z: 4, core: 2. Of those that a mesh axis runs over, the one named last changes fastest.
Arguments:
- tokens: bfloat16 [8192, 1024], P(('rep', 'shard')), may hold values from -6 to 6
- prefix: int32 [32], P(('rep', 'shard')), may hold values from 25 to 128
- routes: int32 [8192, 8], P(('rep', 'shard')), may hold values from 0 to 31, all different within a row; in each aligned block of 256 rows (0 to 255, 256 to 511, ...) at most 96 rows name the same one
- cotangent: bfloat16 [8192, 1024], P(('rep', 'shard')), may hold values from -6 to 6
- w_query: bfloat16 [1024, 1024], P('shard'), may hold values from -0.625 to 0.625
- key_weight: bfloat16 [1024, 512], P('shard'), may hold values from -0.625 to 0.625
- value_weight: bfloat16 [1024, 512], P('shard'), may hold values from -0.1875 to 0.1875
- w_out: bfloat16 [1024, 1024], P('shard'), may hold values from -6 to 6
- norm_attn: bfloat16 [1024], P('shard'), may hold values from 0.5 to 1.5
- norm_moe: bfloat16 [1024], P('shard'), may hold values from 0.5 to 1.5
- w_router: bfloat16 [1024, 32], P('shard'), may hold values from -0.09375 to 0.09375
- w_gate: bfloat16 [32, 1024, 512], P('shard'), may hold values from -0.1875 to 0.1875
- w_up: bfloat16 [32, 1024, 512], P('shard'), may hold values from -0.1875 to 0.1875
- w_down: bfloat16 [32, 512, 1024], P('shard'), may hold values from -6 to 6
Outputs:
- layer_out: bfloat16 [8192, 1024], P(('rep', 'shard'))
- d_tokens: float32 [8192, 1024], P(('rep', 'shard'))
- d_w_query: float32 [1024, 1024], P('shard')
- d_w_key: float32 [1024, 512], P('shard')
- d_w_value: float32 [1024, 512], P('shard')
- d_w_out: float32 [1024, 1024], P('shard')
- d_norm_attn: float32 [1024], P('shard')
- d_norm_moe: float32 [1024], P('shard')
- d_w_router: float32 [1024, 32], P('shard')
- d_w_gate: float32 [32, 1024, 512], P('shard')
- d_w_up: float32 [32, 1024, 512], P('shard')
- d_w_down: float32 [32, 512, 1024], P('shard')
Inputs may be any that keep to these rules, and one draw needn't show every extreme that they name: `routes`: each row names 8 different experts; among the rows of one device no expert is named more than 96 times, and in every draw some device's rows name some expert exactly 96 times.
All inputs are finite; a program needn't handle non-finite values.
Results may differ from a plain program's by a relative error of at most 0.024.
Values may be sent and summed in bfloat16 or wider, within the bound.
A program may use at most 256 MiB of HBM per device.

v0:
```python
import math
import jax
import jax.numpy as jnp
from jax import lax
from jax.sharding import PartitionSpec as P

QUERY_HEADS = 16
KEY_VALUE_HEADS = 8
HEAD_SIZE = 64
CAP = 96
LANES = 128
MOST_GATHERED = 4
epsilon = 1e-06
score_scale = 0.015625
branch_scale = 0.22
masked_value = -1e30
f32 = jnp.float32
bf16 = jnp.bfloat16


def dot(left, right, contract=((1,), (0,))):
    return lax.dot_general(left, right, (contract, ((), ())), preferred_element_type=f32)


def norm_scale(rows):
    return lax.rsqrt(jnp.mean(rows * rows, axis=-1, keepdims=True) + epsilon)


def norm_backward(rows, scaling, gain, upstream):
    weighted = upstream * gain
    inner_mean = jnp.mean(weighted * rows, axis=-1, keepdims=True)
    gradient = scaling * weighted - rows * (scaling * scaling * scaling) * inner_mean
    return (gradient, jnp.sum(upstream * rows * scaling, axis=0, keepdims=True))


def rotary_tables(count):
    half = HEAD_SIZE // 2
    places = jnp.arange(count, dtype=f32)
    inverse = jnp.exp(jnp.arange(half, dtype=f32) * (-2.0 * math.log(10000.0) / HEAD_SIZE))
    angles = places[:, None] * inverse[None, :]
    return (jnp.cos(angles)[:, None, :], jnp.sin(angles)[:, None, :])


def apply_rotary(rows, cosine, sine):
    half = HEAD_SIZE // 2
    shaped = rows.reshape(rows.shape[0], -1, HEAD_SIZE)
    first, second = (shaped[..., :half], shaped[..., half:])
    turned = jnp.concatenate(
        [first * cosine - second * sine, second * cosine + first * sine], axis=-1
    )
    return turned.reshape(rows.shape)


def attention_scores(query, keys, prefix_len):
    count = query.shape[0]
    raw = jnp.einsum("tngd,snd->ngts", query, keys, preferred_element_type=f32)
    place = jnp.arange(count, dtype=jnp.int32)
    visible = (place[None, :] <= place[:, None]) | (place[None, :] < prefix_len)
    return jnp.where(visible, raw * score_scale, masked_value)


def slots_of(gates, first_expert, local):
    tokens = gates.shape[1]
    mine = lax.dynamic_slice_in_dim(gates, first_expert, local, axis=2)
    named = mine > 0
    place = jnp.arange(tokens)
    earlier = (place[None, :] < place[:, None]).astype(bf16)
    rank = jnp.einsum("ts,bsl->blt", earlier, named.astype(bf16), preferred_element_type=f32)
    slot = jnp.arange(CAP, dtype=f32)
    here = (rank[:, :, None, :] == slot[None, None, :, None]) & named.transpose(0, 2, 1)[
        :, :, None, :
    ]
    return (here, mine)


def body(
    tokens,
    prefix,
    routes,
    cotangent,
    w_query,
    key_weight,
    value_weight,
    w_out,
    norm_attn,
    norm_moe,
    w_router,
    w_gate,
    w_up,
    w_down,
):
    inputs = tokens.astype(f32)
    count, width = inputs.shape
    local, _, hidden = w_gate.shape
    shards, reps = (lax.axis_size("shard"), lax.axis_size("rep"))
    experts = local * shards
    kv_width = key_weight.shape[1]
    me, rep = (lax.axis_index("shard"), lax.axis_index("rep"))
    group = QUERY_HEADS // KEY_VALUE_HEADS
    small = jnp.concatenate([w_router, norm_attn[:, None], norm_moe[:, None]], axis=1)
    small = jnp.pad(small, ((0, 0), (0, LANES - small.shape[1])))
    packed = jnp.concatenate([w_query, key_weight, value_weight, w_out, small], axis=1)
    packed = lax.all_gather(packed, "shard", axis=0, tiled=True)
    cuts = [width, width + kv_width, width + 2 * kv_width, 2 * width + 2 * kv_width]
    wq, wk, wv, wo, small = jnp.split(packed, cuts, axis=1)
    wr = small[:, :experts]
    gain_one = small[:, experts].astype(f32)[None, :]
    gain_two = small[:, experts + 1].astype(f32)[None, :]
    spread = reps <= MOST_GATHERED
    axes = ("rep", "shard") if spread else "shard"
    all_cot = lax.all_gather(cotangent, axes, axis=0, tiled=True)
    scale_one = norm_scale(inputs)
    normed_one = (inputs * scale_one * gain_one).astype(bf16)
    cosine, sine = rotary_tables(count)
    query = apply_rotary(dot(normed_one, wq), cosine, sine).astype(bf16)
    keys = apply_rotary(dot(normed_one, wk), cosine, sine).astype(bf16)
    values = dot(normed_one, wv).astype(bf16)
    query4 = query.reshape(count, KEY_VALUE_HEADS, group, HEAD_SIZE)
    keys3 = keys.reshape(count, KEY_VALUE_HEADS, HEAD_SIZE)
    values3 = values.reshape(count, KEY_VALUE_HEADS, HEAD_SIZE)
    scores = attention_scores(query4, keys3, prefix[0])
    weights = jnp.exp(scores - jnp.max(scores, axis=-1, keepdims=True))
    probs = weights / jnp.sum(weights, axis=-1, keepdims=True)
    probs_low = probs.astype(bf16)
    attended = jnp.einsum("ngts,snd->tngd", probs_low, values3, preferred_element_type=f32)
    attended = attended.reshape(count, -1).astype(bf16)
    hidden_one = inputs + branch_scale * dot(attended, wo)
    scale_two = norm_scale(hidden_one)
    normed_two = (hidden_one * scale_two * gain_two).astype(bf16)
    logits = dot(normed_two, wr)
    picks = routes[:, :, None] == jnp.arange(experts, dtype=jnp.int32)[None, None, :]
    chosen_mask = jnp.any(picks, axis=1)
    top = jnp.max(jnp.where(chosen_mask, logits, -jnp.inf), axis=1, keepdims=True)
    gates = jnp.where(chosen_mask, jnp.exp(logits - top), 0.0)
    gates = gates / jnp.sum(gates, axis=1, keepdims=True)
    high = gates.astype(bf16)
    low = (gates - high.astype(f32)).astype(bf16)
    pad = jnp.zeros((count, LANES - 2 * experts), bf16)
    sent = jnp.concatenate([normed_two, high, low, pad], axis=1)
    arrived = lax.all_gather(sent, axes, axis=0, tiled=True)
    arrived = arrived.reshape(-1, shards, count, width + LANES)
    all_gates = arrived[..., width : width + experts].astype(f32)
    all_gates = all_gates + arrived[..., width + experts : width + 2 * experts].astype(f32)
    all_cot = all_cot.reshape(-1, shards, count, width)

    def gathered(number):
        rows = lax.dynamic_index_in_dim(arrived, number, 0, keepdims=False)[..., :width]
        cot = lax.dynamic_index_in_dim(all_cot, number, 0, keepdims=False)
        gate_rows = lax.dynamic_index_in_dim(all_gates, number, 0, keepdims=False)
        here, mine = slots_of(gate_rows, me * local, local)
        one_hot = here.astype(bf16)
        slot_gate = jnp.sum(jnp.where(here, mine.transpose(0, 2, 1)[:, :, None, :], 0.0), axis=3)
        xg = jnp.einsum("blst,btd->lbsd", one_hot, rows).reshape(local, -1, width)
        cg = jnp.einsum("blst,btd->lbsd", one_hot, cot).reshape(local, -1, width)
        scale = branch_scale * slot_gate.transpose(1, 0, 2).reshape(local, -1)[:, :, None]
        gate_part = jnp.einsum("lmd,ldf->lmf", xg, w_gate, preferred_element_type=f32)
        up_part = jnp.einsum("lmd,ldf->lmf", xg, w_up, preferred_element_type=f32)
        raw = jnp.einsum("lmd,lfd->lmf", cg, w_down, preferred_element_type=f32)
        sigma = jax.nn.sigmoid(gate_part)
        act = gate_part * sigma
        inner = act * up_part
        d_inner = raw * scale
        d_gate = (d_inner * up_part * sigma * (1.0 + gate_part * (1.0 - sigma))).astype(bf16)
        d_up = (d_inner * act).astype(bf16)
        scaled = (inner * scale).astype(bf16)
        sums = (
            jnp.einsum("lmd,lmf->ldf", xg, d_gate, preferred_element_type=f32),
            jnp.einsum("lmd,lmf->ldf", xg, d_up, preferred_element_type=f32),
            jnp.einsum("lmf,lmd->lfd", scaled, cg, preferred_element_type=f32),
        )
        return (sums, (one_hot, inner, raw, d_gate, d_up, scaled))

    sums, (one_hot, inner, raw, d_gate, d_up, scaled) = gathered(rep if spread else 0)
    out_rows = jnp.einsum("lmf,lfd->lmd", scaled, w_down, preferred_element_type=f32).astype(bf16)
    d_rows = jnp.einsum("lmf,ldf->lmd", d_gate, w_gate, preferred_element_type=f32)
    d_rows = (d_rows + jnp.einsum("lmf,ldf->lmd", d_up, w_up, preferred_element_type=f32)).astype(
        bf16
    )
    slot_d_gate = branch_scale * jnp.sum(inner * raw, axis=2)
    shape4 = (local, shards, CAP, width)
    mix = jnp.einsum(
        "blst,lbsd->btd", one_hot, out_rows.reshape(shape4), preferred_element_type=f32
    )
    d_in = jnp.einsum("blst,lbsd->btd", one_hot, d_rows.reshape(shape4), preferred_element_type=f32)
    dg_local = jnp.sum(
        jnp.where(
            one_hot > 0, slot_d_gate.reshape(local, shards, CAP).transpose(1, 0, 2)[..., None], 0.0
        ),
        axis=2,
    )
    dg = jnp.zeros((shards, count, LANES), f32)
    dg = lax.dynamic_update_slice(dg, dg_local.transpose(0, 2, 1), (0, 0, me * local))
    back = jnp.concatenate([mix, d_in, dg], axis=2).astype(bf16).reshape(shards * count, -1)
    back = lax.psum_scatter(back, "shard", scatter_dimension=0, tiled=True).astype(f32)
    if spread:
        for step in range(1, reps):
            more, _ = gathered(lax.rem(rep + step, reps))
            sums = tuple((a + b for a, b in zip(sums, more)))
    else:
        sums = tuple((lax.psum(a.astype(bf16), "rep").astype(f32) for a in sums))
    d_w_gate, d_w_up, d_w_down = sums
    result = (hidden_one + back[:, :width]).astype(bf16)
    cot = cotangent.astype(f32)
    d_gates = back[:, 2 * width : 2 * width + experts]
    d_logits = gates * (d_gates - jnp.sum(gates * d_gates, axis=1, keepdims=True))
    d_logits = d_logits.astype(bf16)
    d_router = dot(normed_two, d_logits, ((0,), (0,)))
    d_normed_two = back[:, width : 2 * width] + dot(d_logits, wr, ((1,), (1,)))
    d_hidden, d_gain_two = norm_backward(hidden_one, scale_two, gain_two, d_normed_two)
    d_hidden = d_hidden + cot
    d_projected = (branch_scale * d_hidden).astype(bf16)
    d_wo = dot(attended, d_projected, ((0,), (0,)))
    d_attended = dot(d_projected, wo, ((1,), (1,))).astype(bf16)
    d_attended = d_attended.reshape(count, KEY_VALUE_HEADS, group, HEAD_SIZE)
    d_values = jnp.einsum("ngts,tngd->snd", probs_low, d_attended, preferred_element_type=f32)
    d_probs = jnp.einsum("tngd,snd->ngts", d_attended, values3, preferred_element_type=f32)
    weighted = jnp.sum(probs * d_probs, axis=-1, keepdims=True)
    d_scores = (probs * (d_probs - weighted) * score_scale).astype(bf16)
    d_query = jnp.einsum("ngts,snd->tngd", d_scores, keys3, preferred_element_type=f32)
    d_keys = jnp.einsum("ngts,tngd->snd", d_scores, query4, preferred_element_type=f32)
    d_query = apply_rotary(d_query.reshape(count, -1), cosine, -sine).astype(bf16)
    d_keys = apply_rotary(d_keys.reshape(count, -1), cosine, -sine).astype(bf16)
    d_values = d_values.reshape(count, -1).astype(bf16)
    d_qkv = jnp.concatenate([d_query, d_keys, d_values], axis=1)
    d_w_qkv = dot(normed_one, d_qkv, ((0,), (0,)))
    d_normed_one = dot(d_qkv, packed[:, : cuts[2]], ((1,), (1,)))
    d_tokens, d_gain_one = norm_backward(inputs, scale_one, gain_one, d_normed_one)
    d_tokens = d_tokens + d_hidden
    small = jnp.concatenate([d_router, d_gain_one.T, d_gain_two.T], axis=1)
    small = jnp.pad(small, ((0, 0), (0, LANES - small.shape[1])))
    shares = jnp.concatenate([d_w_qkv, d_wo, small], axis=1).astype(bf16)
    shares = lax.psum_scatter(shares, "shard", scatter_dimension=0, tiled=True)
    totals = lax.psum(shares, "rep").astype(f32)
    d_wq, d_wk, d_wv, d_wo, small = jnp.split(totals, cuts, axis=1)
    return (
        result,
        d_tokens,
        d_wq,
        d_wk,
        d_wv,
        d_wo,
        small[:, experts],
        small[:, experts + 1],
        small[:, :experts],
        d_w_gate,
        d_w_up,
        d_w_down,
    )


def solution(mesh):
    rows = P(("rep", "shard"), None)
    one, two, three = (P("shard"), P("shard", None), P("shard", None, None))
    return jax.shard_map(
        body,
        mesh=mesh,
        in_specs=(
            rows,
            P(("rep", "shard")),
            rows,
            rows,
            two,
            two,
            two,
            two,
            one,
            one,
            two,
            three,
            three,
            three,
        ),
        out_specs=(rows, rows, two, two, two, two, one, one, two, three, three, three),
        check_vma=False,
    )
```

profile of v0, /device:TPU:0, one launch (start us, length us, event | category | flops | bytes accessed | tf_op | source)
XLA Modules:
  0.0 835.5 jit_solution(13934311828291077232)
XLA Ops:
  17.2 45.2 %all-gather.4.cloned.1.call-done = bf16[1024,3200]{1,0:T(8,128)(2,1)} async-done(((bf16[128,3200]{1,0:T(8,128)(2,1)}), bf16[1024,3200]{1,0:T(8,128)(2,1)}) %all-gather.4.cloned.1.call-update) | async-done | bytes 6553616 | tf_op jit(solution)/shard_map/all_gather | solution.py:103
  85.2 124.0 %all-gather.6.cloned.1.call-done = bf16[8192,1152]{1,0:T(8,128)(2,1)} async-done(((bf16[256,1152]{1,0:T(8,128)(2,1)}), bf16[8192,1152]{1,0:T(8,128)(2,1)}) %all-gather.6.cloned.1.call-update) | async-done | bytes 18874384 | tf_op jit(solution)/shard_map/all_gather | solution.py:140
  218.9 13.0 %dynamic-slice_bitcast_fusion = (bf16[8,256,1152]{2,1,0:T(8,128)(2,1)}, bf16[8,256,1152]{2,1,0:T(8,128)(2,1)S(1)}, bf16[8,256,1152]{2,1,0:T(8,128)(2,1)}, bf16[8,256,1152]{2,1,0:T(8,128)(2,1)}) fusion(bf16[4,8,256,1152]{3,2,1,0:T(8,128)(2,1)} %bitcast.302, s32[]{:T(128)S(6)} %select_n.86, s32[]{:T(128)S(6)} %select_n.83, s32[]{:T(128)S(6)} %select_n.80, ...), kind=kLoop, calls=%fused_computation.37 | loop fusion | bytes 37748752 | tf_op jit(solution)/shard_map/jit(dynamic_index_in_dim)/squeeze | solution.py:147
  237.4 87.7 %all-gather.8.cloned.1.call-done = bf16[8192,1024]{1,0:T(8,128)(2,1)} async-done(((bf16[256,1024]{1,0:T(8,128)(2,1)}), bf16[8192,1024]{1,0:T(8,128)(2,1)}) %all-gather.8.cloned.1.call-update) | async-done | bytes 16777232 | tf_op jit(solution)/shard_map/all_gather | solution.py:111
  352.8 8.8 %fusion.239 = f32[4,768,512]{1,2,0:T(8,128)} fusion(bf16[4,768,1024]{2,1,0:T(8,128)(2,1)} %bitcast.319, bf16[4,1024,512]{2,1,0:T(8,128)(2,1)S(1)} %copy-done.9), kind=kOutput, calls=%fused_computation.296 | convolution fusion | flops 3221225472 | bytes 16777216 | tf_op jit(solution)/shard_map/lmd,ldf->lmf/dot_general | solution.py:156
  361.6 8.4 %fusion.241 = f32[4,768,512]{1,2,0:T(8,128)} fusion(bf16[4,768,1024]{2,1,0:T(8,128)(2,1)S(1)} %bitcast.308, bf16[4,1024,512]{2,1,0:T(8,128)(2,1)} %param.26), kind=kOutput, calls=%fused_computation.298 | convolution fusion | flops 3221225472 | bytes 16777216 | tf_op jit(solution)/shard_map/lmd,ldf->lmf/dot_general | solution.py:157
  370.0 10.2 %fusion.238 = f32[4,768,512]{1,2,0:T(8,128)} fusion(bf16[4,768,1024]{2,1,0:T(8,128)(2,1)} %bitcast.320, bf16[4,1024,512]{2,1,0:T(8,128)(2,1)} %param.26), kind=kOutput, calls=%fused_computation.295 | convolution fusion | flops 3221225472 | bytes 16777216 | tf_op jit(solution)/shard_map/lmd,ldf->lmf/dot_general | solution.py:157
  395.7 10.9 %fusion.230 = f32[4,768,512]{1,2,0:T(8,128)} fusion(bf16[4,768,1024]{2,1,0:T(8,128)(2,1)S(1)} %bitcast.295, bf16[4,1024,512]{2,1,0:T(8,128)(2,1)} %param.26), kind=kOutput, calls=%fused_computation.287 | convolution fusion | flops 3221225472 | bytes 16777216 | tf_op jit(solution)/shard_map/lmd,ldf->lmf/dot_general | solution.py:157
  438.3 15.0 %multiply_reduce_fusion = (f32[4,768]{1,0:T(4,128)S(1)}, f32[4,768,512]{1,2,0:T(8,128)}) fusion(f32[4,768,512]{1,2,0:T(8,128)} %fusion.230, f32[4,768,512]{1,2,0:T(8,128)} %fusion.229, bf16[4,768,1024]{2,1,0:T(8,128)(2,1)S(1)} %bitcast.299, bf16[4,512,1024]{2,1,0:T(8,128)(2,1)} %param.27), kind=kOutput, calls=%fused_computation.31 | convolution fusion | flops 3232232448 | bytes 29372416 | tf_op jit(solution)/shard_map/lmd,lfd->lmf/dot_general | solution.py:158
  456.7 8.4 %multiply_convert_fusion.11 = (bf16[4,768,512]{1,2,0:T(8,128)(2,1)S(1)}, bf16[4,768,512]{1,2,0:T(8,128)(2,1)S(1)}, bf16[4,768,512]{1,2,0:T(8,128)(2,1)S(1)}) fusion(f32[4,768]{1,0:T(4,128)S(1)} %mul.709, f32[4,768,512]{1,2,0:T(8,128)} %fusion.230, f32[4,768,512]{1,2,0:T(8,128)} %fusion.229, f32[4,768,512]{1,2,0:T(8,128)} %get-tuple-element.124), kind=kLoop, calls=%fused_computation.34 | loop fusion | flops 26738688 | bytes 28323840 | tf_op jit(solution)/shard_map/convert_element_type | solution.py:165
  470.7 7.3 bitcast_convert_fusion.1
  484.8 9.6 %add_convert_fusion = bf16[4,768,1024]{2,1,0:T(8,128)(2,1)} fusion(f32[4,768,1024]{2,1,0:T(8,128)} %fusion.231, bf16[4,768,512]{1,2,0:T(8,128)(2,1)S(1)} %get-tuple-element.91, bf16[4,1024,512]{2,1,0:T(8,128)(2,1)} %param.26), kind=kOutput, calls=%fused_computation.4 | convolution fusion | flops 3227516928 | bytes 26214400 | tf_op jit(solution)/shard_map/lmf,ldf->lmd/dot_general | solution.py:176
  494.4 7.2 bitcast_convert_fusion
  503.5 7.1 pad_maximum_fusion
  526.4 8.7 %fusion.235 = f32[4,768,512]{1,2,0:T(8,128)} fusion(bf16[4,768,1024]{2,1,0:T(8,128)(2,1)S(1)} %bitcast.328, bf16[4,1024,512]{2,1,0:T(8,128)(2,1)} %param.26), kind=kOutput, calls=%fused_computation.292 | convolution fusion | flops 3221225472 | bytes 16777216 | tf_op jit(solution)/shard_map/lmd,ldf->lmf/dot_general | solution.py:157
  535.2 11.0 %fusion.234 = f32[4,768,512]{1,2,0:T(8,128)} fusion(bf16[4,768,1024]{2,1,0:T(8,128)(2,1)} %bitcast.329, bf16[4,512,1024]{2,1,0:T(8,128)(2,1)} %param.27), kind=kOutput, calls=%fused_computation.291 | convolution fusion | flops 3221225472 | bytes 16777216 | tf_op jit(solution)/shard_map/lmd,lfd->lmf/dot_general | solution.py:158
  546.2 8.4 %fusion.237 = f32[4,768,512]{1,2,0:T(8,128)} fusion(bf16[4,768,1024]{2,1,0:T(8,128)(2,1)} %bitcast.335, bf16[4,512,1024]{2,1,0:T(8,128)(2,1)S(1)} %copy-done.52), kind=kOutput, calls=%fused_computation.294 | convolution fusion | flops 3221225472 | bytes 16777216 | tf_op jit(solution)/shard_map/lmd,lfd->lmf/dot_general | solution.py:158
  560.1 12.0 %fusion.39 = f32[4,512,1024]{2,1,0:T(8,128)} fusion(bf16[4,768,1024]{2,1,0:T(8,128)(2,1)S(1)} %bitcast.334, f32[4,768,512]{1,2,0:T(8,128)} %fusion.241, f32[4,768]{1,0:T(4,128)S(1)} %mul.780, f32[4,768,512]{1,2,0:T(8,128)} %fusion.242), kind=kOutput, calls=%fused_computation.79 | convolution fusion | flops 3232235520 | bytes 27275264 | tf_op jit(solution)/shard_map/lmf,lmd->lfd/dot_general | solution.py:169
  572.0 13.2 %fusion.38 = f32[4,512,1024]{2,1,0:T(8,128)} fusion(bf16[4,768,1024]{2,1,0:T(8,128)(2,1)} %bitcast.336, f32[4,768,512]{1,2,0:T(8,128)} %fusion.238, f32[4,768]{1,0:T(4,128)S(1)} %copy-done.45, f32[4,768,512]{1,2,0:T(8,128)} %fusion.239), kind=kOutput, calls=%fused_computation.78 | convolution fusion | flops 3232235520 | bytes 27275264 | tf_op jit(solution)/shard_map/lmf,lmd->lfd/dot_general | solution.py:169
  585.3 14.5 %fusion.35 = f32[4,1024,512]{2,1,0:T(8,128)} fusion(bf16[4,768,1024]{2,1,0:T(8,128)(2,1)} %bitcast.321, f32[4,768,512]{1,2,0:T(8,128)} %fusion.237, f32[4,768]{1,0:T(4,128)S(1)} %copy-done.45, f32[4,768,512]{1,2,0:T(8,128)} %fusion.239), kind=kOutput, calls=%fused_computation.75 | convolution fusion | flops 3232235520 | bytes 27275264 | tf_op jit(solution)/shard_map/lmd,lmf->ldf/dot_general | solution.py:168
  599.8 14.7 %fusion.36 = f32[4,1024,512]{2,1,0:T(8,128)} fusion(bf16[4,768,1024]{2,1,0:T(8,128)(2,1)} %bitcast.309, f32[4,768,512]{1,2,0:T(8,128)} %fusion.240, f32[4,768]{1,0:T(4,128)S(1)} %mul.780, f32[4,768,512]{1,2,0:T(8,128)} %fusion.242), kind=kOutput, calls=%fused_computation.76 | convolution fusion | flops 3232235520 | bytes 27275264 | tf_op jit(solution)/shard_map/lmd,lmf->ldf/dot_general | solution.py:168
  614.5 14.4 %fusion.34 = f32[4,1024,512]{2,1,0:T(8,128)} fusion(bf16[4,768,1024]{2,1,0:T(8,128)(2,1)} %bitcast.323, f32[4,768,512]{1,2,0:T(8,128)} %fusion.234, f32[4,768]{1,0:T(4,128)S(1)} %copy-done.43, f32[4,768,512]{1,2,0:T(8,128)} %fusion.236), kind=kOutput, calls=%fused_computation.74 | convolution fusion | flops 3232235520 | bytes 27275264 | tf_op jit(solution)/shard_map/lmd,lmf->ldf/dot_general | solution.py:168
  644.4 8.0 fusion.144
  652.4 8.2 fusion.111
  678.4 14.6 %fusion.37 = f32[4,512,1024]{2,1,0:T(8,128)} fusion(bf16[4,768,1024]{2,1,0:T(8,128)(2,1)} %bitcast.330, f32[4,768,512]{1,2,0:T(8,128)} %fusion.235, f32[4,768]{1,0:T(4,128)S(1)} %copy-done.44, f32[4,768,512]{1,2,0:T(8,128)} %fusion.236), kind=kOutput, calls=%fused_computation.77 | convolution fusion | flops 3232235520 | bytes 27275264 | tf_op jit(solution)/shard_map/lmf,lmd->lfd/dot_general | solution.py:169
  693.1 9.8 %fusion.233 = f32[4,1024,512]{2,1,0:T(8,128)} fusion(bf16[4,768,1024]{2,1,0:T(8,128)(2,1)} %bitcast.297, bf16[4,768,512]{1,2,0:T(8,128)(2,1)S(1)} %copy-done.6), kind=kOutput, calls=%fused_computation.290 | convolution fusion | flops 3221225472 | bytes 17825792 | tf_op jit(solution)/shard_map/lmd,lmf->ldf/dot_general | solution.py:167
  702.8 17.3 %fusion.47 = f32[4,1024,512]{2,1,0:T(8,128)} fusion(bf16[4,768,1024]{2,1,0:T(8,128)(2,1)} %bitcast.322, f32[4,768,512]{1,2,0:T(8,128)} %fusion.239, f32[4,768,512]{1,2,0:T(8,128)} %fusion.238, f32[4,768,512]{1,2,0:T(8,128)} %fusion.237, f32[4,768]{1,0:T(4,128)S(1)} %copy-done.46), kind=kOutput, calls=%fused_computation.96 | convolution fusion | flops 3238526976 | bytes 33566720 | tf_op jit(solution)/shard_map/lmd,lmf->ldf/dot_general | solution.py:167
  720.2 17.0 %fusion.46 = f32[4,1024,512]{2,1,0:T(8,128)} fusion(bf16[4,768,1024]{2,1,0:T(8,128)(2,1)} %bitcast.324, f32[4,768,512]{1,2,0:T(8,128)} %fusion.236, f32[4,768,512]{1,2,0:T(8,128)} %fusion.235, f32[4,768,512]{1,2,0:T(8,128)} %fusion.234, f32[4,768]{1,0:T(4,128)S(1)} %copy-done.44), kind=kOutput, calls=%fused_computation.95 | convolution fusion | flops 3238526976 | bytes 33566720 | tf_op jit(solution)/shard_map/lmd,lmf->ldf/dot_general | solution.py:167
  737.2 15.8 %add_add_fusion = f32[4,512,1024]{2,1,0:T(8,128)} fusion(f32[4,512,1024]{2,1,0:T(8,128)} %fusion.39, f32[4,512,1024]{2,1,0:T(8,128)} %fusion.38, f32[4,512,1024]{2,1,0:T(8,128)} %fusion.37, bf16[4,768,512]{1,2,0:T(8,128)(2,1)S(1)} %copy-done.8, bf16[4,768,1024]{2,1,0:T(8,128)(2,1)} %bitcast.300), kind=kOutput, calls=%fused_computation.8 | convolution fusion | flops 3227516928 | bytes 42991616 | tf_op jit(solution)/shard_map/lmf,lmd->lfd/dot_general | solution.py:169
  753.0 21.8 %add_add_fusion.2 = f32[4,1024,512]{2,1,0:T(8,128)} fusion(f32[4,1024,512]{2,1,0:T(8,128)} %fusion.47, f32[4,1024,512]{2,1,0:T(8,128)} %fusion.233, f32[4,1024,512]{2,1,0:T(8,128)} %fusion.46, bf16[4,768,1024]{2,1,0:T(8,128)(2,1)} %bitcast.310, f32[4,768,512]{1,2,0:T(8,128)} %fusion.242, f32[4,768,512]{1,2,0:T(8,128)} %fusion.241, ...), kind=kOutput, calls=%fused_computation.10 | convolution fusion | flops 3244818432 | bytes 58732544 | tf_op jit(solution)/shard_map/lmd,lmf->ldf/dot_general | solution.py:167
  774.8 15.5 %add_add_fusion.1 = f32[4,1024,512]{2,1,0:T(8,128)} fusion(f32[4,1024,512]{2,1,0:T(8,128)} %fusion.36, f32[4,1024,512]{2,1,0:T(8,128)} %fusion.35, f32[4,1024,512]{2,1,0:T(8,128)} %fusion.34, bf16[4,768,1024]{2,1,0:T(8,128)(2,1)} %bitcast.298, bf16[4,768,512]{1,2,0:T(8,128)(2,1)S(1)} %copy-done.3), kind=kOutput, calls=%fused_computation.9 | convolution fusion | flops 3227516928 | bytes 42991616 | tf_op jit(solution)/shard_map/lmd,lmf->ldf/dot_general | solution.py:168
  793.3 27.6 %all-reduce.4.cloned.1.call-done = bf16[128,3200]{1,0:T(8,128)(2,1)} async-done(((bf16[128,3200]{1,0:T(8,128)(2,1)}), bf16[128,3200]{1,0:T(8,128)(2,1)}) %all-reduce.4.cloned.1.call-update) | async-done | bytes 819216 | tf_op jit(solution)/shard_map/psum | solution.py:233
  (291 shorter events, 203.9 us)
Async XLA Ops:
  7.2 58.7 %copy-start.19 = (bf16[256,1024]{1,0:T(8,128)(2,1)S(1)}, bf16[256,1024]{1,0:T(8,128)(2,1)}, u32[]{:S(2)}) copy-start(bf16[256,1024]{1,0:T(8,128)(2,1)} %param.14) | copy-start | bytes 1572868
  7.2 55.2 %all-gather.4.cloned.1.call-start = ((), (), s32[]{:S(2)}) async-start(), calls=%async_computation.2 | async-start | bytes 7372800 | tf_op jit(solution)/shard_map/all_gather | solution.py:103
  12.9 196.3 %all-gather.6.cloned.1.call-start = ((), (), s32[]{:S(2)}) async-start(), calls=%async_computation.3 | async-start | bytes 19464192 | tf_op jit(solution)/shard_map/all_gather | solution.py:140
  16.3 54.5 %copy-start.48 = (f32[256]{0:T(256)}, f32[256]{0:T(256)S(1)}, u32[]{:S(2)}) copy-start(f32[256]{0:T(256)S(1)} %get-tuple-element.111) | copy-start | bytes 3076
  17.2 53.5 %copy-start.25 = (f32[256,32]{0,1:T(8,128)}, f32[256,32]{0,1:T(8,128)S(1)}, u32[]{:S(2)}) copy-start(f32[256,32]{0,1:T(8,128)S(1)} %get-tuple-element.116) | copy-start | bytes 98308
  63.8 16.5 %copy-start.37 = (f32[1024]{0:T(1024)}, f32[1024]{0:T(1024)S(1)}, u32[]{:S(2)}) copy-start(f32[1024]{0:T(1024)S(1)} %get-tuple-element.72) | copy-start | bytes 12292
  80.3 128.9 %copy-start.41 = (f32[256]{0:T(256)}, f32[256]{0:T(256)S(1)}, u32[]{:S(2)}) copy-start(f32[256]{0:T(256)S(1)} %get-tuple-element.113) | copy-start | bytes 3076
  80.8 134.1 %copy-start.15 = (bf16[256,1024]{1,0:T(8,128)(2,1)}, bf16[256,1024]{1,0:T(8,128)(2,1)S(1)}, u32[]{:S(2)}) copy-start(bf16[256,1024]{1,0:T(8,128)(2,1)S(1)} %multiply_convert_fusion.24) | copy-start | bytes 1572868
  84.3 240.8 %all-gather.8.cloned.1.call-start = ((), (), s32[]{:S(2)}) async-start(), calls=%async_computation.4 | async-start | bytes 17301504 | tf_op jit(solution)/shard_map/all_gather | solution.py:111
  85.1 543.8 %reduce-scatter.3.cloned.1.call-start = ((), (), s32[]{:S(2)}) async-start(), calls=%async_computation.5 | async-start | bytes 10027008 | tf_op jit(solution)/shard_map/reduce_scatter | solution.py:194
  325.1 13.6 %slice-start.10 = ((s8[4718592]{0:T(1024)(128)(4,1)}), s8[4194304]{0:T(1024)(128)(4,1)S(1)}, s32[]{:S(2)}) async-start(s8[4718592]{0:T(1024)(128)(4,1)} %bitcast.340), calls=%async_computation.18 | async-start | bytes 8388608
  347.3 14.3 %copy-start.4 = (bf16[4,8,96,1024]{3,2,1,0:T(8,128)(2,1)}, bf16[4,8,96,1024]{3,2,1,0:T(8,128)(2,1)S(1)}, u32[]{:S(2)}) copy-start(bf16[4,8,96,1024]{3,2,1,0:T(8,128)(2,1)S(1)} %copy.419) | copy-start | bytes 18874372
  395.7 10.9 %copy-start = (bf16[4,8,96,1024]{3,2,1,0:T(8,128)(2,1)}, bf16[4,8,96,1024]{3,2,1,0:T(8,128)(2,1)S(1)}, u32[]{:S(2)}) copy-start(bf16[4,8,96,1024]{3,2,1,0:T(8,128)(2,1)S(1)} %copy.369) | copy-start | bytes 18874372
  438.3 15.0 %copy-start.1 = (bf16[4,8,96,1024]{3,2,1,0:T(8,128)(2,1)}, bf16[4,8,96,1024]{3,2,1,0:T(8,128)(2,1)S(1)}, u32[]{:S(2)}) copy-start(bf16[4,8,96,1024]{3,2,1,0:T(8,128)(2,1)S(1)} %copy.376) | copy-start | bytes 18874372
  465.1 13.0 %copy-start.5 = (bf16[4,768,512]{1,2,0:T(8,128)(2,1)}, bf16[4,768,512]{1,2,0:T(8,128)(2,1)S(1)}, u32[]{:S(2)}) copy-start(bf16[4,768,512]{1,2,0:T(8,128)(2,1)S(1)} %get-tuple-element.90) | copy-start | bytes 9437188
  465.1 19.7 %copy-start.2 = (bf16[4,768,512]{1,2,0:T(8,128)(2,1)}, bf16[4,768,512]{1,2,0:T(8,128)(2,1)S(1)}, u32[]{:S(2)}) copy-start(bf16[4,768,512]{1,2,0:T(8,128)(2,1)S(1)} %get-tuple-element.91) | copy-start | bytes 9437188
  510.7 264.1 %reduce-scatter.5.cloned.1.call-start = ((), (), s32[]{:S(2)}) async-start(), calls=%async_computation.6 | async-start | bytes 7372800 | tf_op jit(solution)/shard_map/reduce_scatter | solution.py:232
  535.2 11.0 %copy-start.52 = (bf16[4,512,1024]{2,1,0:T(8,128)(2,1)S(1)}, bf16[4,512,1024]{2,1,0:T(8,128)(2,1)}, u32[]{:S(2)}) copy-start(bf16[4,512,1024]{2,1,0:T(8,128)(2,1)} %param.27) | copy-start | bytes 12582916
  535.2 19.4 %slice-start.6 = ((s8[6291456]{0:T(1024)(128)(4,1)}), s8[4194304]{0:T(1024)(128)(4,1)S(1)}, s32[]{:S(2)}) async-start(s8[6291456]{0:T(1024)(128)(4,1)} %bitcast.331), calls=%async_computation.14 | async-start | bytes 8388608
  560.1 12.0 %copy-start.45 = (f32[4,768]{1,0:T(4,128)S(1)}, f32[4,768]{1,0:T(4,128)}, u32[]{:S(2)}) copy-start(f32[4,768]{1,0:T(4,128)} %mul.771) | copy-start | bytes 36868
  599.8 14.7 %copy-start.43 = (f32[4,768]{1,0:T(4,128)S(1)}, f32[4,768]{1,0:T(4,128)}, u32[]{:S(2)}) copy-start(f32[4,768]{1,0:T(4,128)} %mul.762) | copy-start | bytes 36868
  614.5 15.9 %copy-start.22 = (f32[256,32]{1,0:T(8,128)S(1)}, f32[256,32]{1,0:T(8,128)}, u32[]{:S(2)}) copy-start(f32[256,32]{1,0:T(8,128)} %get-tuple-element.84) | copy-start | bytes 98308
  614.5 16.2 %copy-start.16 = (bf16[256,1024]{1,0:T(8,128)(2,1)S(1)}, bf16[256,1024]{1,0:T(8,128)(2,1)}, u32[]{:S(2)}) copy-start(bf16[256,1024]{1,0:T(8,128)(2,1)} %copy-done.15) | copy-start | bytes 1572868
  614.5 16.4 %copy-start.14 = (f32[256,1024]{1,0:T(8,128)S(1)}, f32[256,1024]{1,0:T(8,128)}, u32[]{:S(2)}) copy-start(f32[256,1024]{1,0:T(8,128)} %copy-done.13) | copy-start | bytes 3145732
  614.5 16.4 %copy-start.38 = (f32[1024]{0:T(1024)S(1)}, f32[1024]{0:T(1024)}, u32[]{:S(2)}) copy-start(f32[1024]{0:T(1024)} %copy-done.37) | copy-start | bytes 12292
  614.5 16.4 %copy-start.42 = (f32[256]{0:T(256)S(1)}, f32[256]{0:T(256)}, u32[]{:S(2)}) copy-start(f32[256]{0:T(256)} %copy-done.41) | copy-start | bytes 3076
  652.4 10.5 %copy-start.20 = (bf16[256,1024]{1,0:T(8,128)(2,1)S(1)}, bf16[256,1024]{1,0:T(8,128)(2,1)}, u32[]{:S(2)}) copy-start(bf16[256,1024]{1,0:T(8,128)(2,1)} %param.14) | copy-start | bytes 1572868
  677.7 15.3 %copy-start.6 = (bf16[4,768,512]{1,2,0:T(8,128)(2,1)S(1)}, bf16[4,768,512]{1,2,0:T(8,128)(2,1)}, u32[]{:S(2)}) copy-start(bf16[4,768,512]{1,2,0:T(8,128)(2,1)} %copy-done.5) | copy-start | bytes 9437188
  677.8 143.1 %all-reduce.4.cloned.1.call-start = ((), (), s32[]{:S(2)}) async-start(), calls=%async_computation.7 | async-start | bytes 1638400 | tf_op jit(solution)/shard_map/psum | solution.py:233
  720.2 17.0 %copy-start.8 = (bf16[4,768,512]{1,2,0:T(8,128)(2,1)S(1)}, bf16[4,768,512]{1,2,0:T(8,128)(2,1)}, u32[]{:S(2)}) copy-start(bf16[4,768,512]{1,2,0:T(8,128)(2,1)} %copy-done.7) | copy-start | bytes 9437188
  753.0 21.8 %copy-start.3 = (bf16[4,768,512]{1,2,0:T(8,128)(2,1)S(1)}, bf16[4,768,512]{1,2,0:T(8,128)(2,1)}, u32[]{:S(2)}) copy-start(bf16[4,768,512]{1,2,0:T(8,128)(2,1)} %copy-done.2) | copy-start | bytes 9437188
  774.8 15.5 %copy-start.47 = (f32[256]{0:T(256)S(1)}, f32[256]{0:T(256)}, u32[]{:S(2)}) copy-start(f32[256]{0:T(256)} %get-tuple-element.110) | copy-start | bytes 3076
  (42 other events, 253.7 us)
Sparse Core Ops, SparseCore 0:
  13.0 49.3 all-gather.3
  84.5 124.6 all-gather.5
  212.0 113.0 all-gather.7
  510.8 74.1 reduce-scatter.2
  677.9 63.5 reduce-scatter.4
  774.9 45.9 all-reduce.3
where the time goes:
time: 844 us; the launch traced here: 835 us
  matrix products  415 us (49%)
  waiting for transfers between devices  285 us (34%)
  local copies, waits for them, and re-layouts  73.7 us (9%)
  other arithmetic  45.3 us (5%)
  between operations  16.3 us (2%)
    all_gather x1, waiting for transfers between devices, body(): arrived = lax.all_gather(sent, axes, axis=0, tiled=True)  124 us
    all_gather x1, waiting for transfers between devices, body(): all_cot = lax.all_gather(cotangent, axes, axis=0, tiled=True)  87.7 us
    dot_general x4, matrix products, gathered(): jnp.einsum('lmd,lmf->ldf', xg, d_gate, preferred_element_type=f32)  65.9 us
    dot_general x4, matrix products, gathered(): jnp.einsum('lmd,lmf->ldf', xg, d_up, preferred_element_type=f32)  59 us
    dot_general x4, matrix products, gathered(): jnp.einsum('lmf,lmd->lfd', scaled, cg, preferred_element_type=f32)  55.6 us
    all_gather x1, waiting for transfers between devices, body(): packed = lax.all_gather(packed, 'shard', axis=0, tiled=True)  45.2 us
    dot_general x4, matrix products, gathered(): raw = jnp.einsum('lmd,lfd->lmf', cg, w_down, preferred_element_type=f32)  39.8 us
    dot_general x4, matrix products, gathered(): up_part = jnp.einsum('lmd,ldf->lmf', xg, w_up, preferred_element_type=f32)  38.2 us
  transfers between devices with their start and end apart: 6, of which 4 were waited for; matrix products, arithmetic and copies ran while one was open for 31% of the time, Pallas kernels for 0%

commit v1 on v0

--- a/solution.py
+++ b/solution.py
@@ -1,3 +1,4 @@
+import functools
 import math
 import jax
 import jax.numpy as jnp
@@ -16,6 +17,27 @@
 masked_value = -1e30
 f32 = jnp.float32
 bf16 = jnp.bfloat16
+
+
+def recover_ratios(s0, along_axis):
+    fan = lax.axis_size(along_axis)
+    passed = range(fan)
+    x_new = map(lambda h: (h, (h + 1) % fan), passed)
+    cards = list(x_new)
+
+    def start_results(tmp):
+        if len(tmp) == fan:
+            return tmp
+        w_next = lax.ppermute(tmp[0], along_axis, cards)
+        return start_results([w_next, *tmp])
+
+    x_next = start_results([s0])
+    k_now = jnp.concatenate(x_next, 0)
+    v_now = lax.axis_index(along_axis)
+    return jnp.roll(k_now, (v_now + 1) * s0.shape[0], 0)
+
+
+table_convert = functools.partial(recover_ratios, along_axis="shard")
 
 
 def dot(left, right, contract=((1,), (0,))):
@@ -100,7 +122,7 @@
     small = jnp.concatenate([w_router, norm_attn[:, None], norm_moe[:, None]], axis=1)
     small = jnp.pad(small, ((0, 0), (0, LANES - small.shape[1])))
     packed = jnp.concatenate([w_query, key_weight, value_weight, w_out, small], axis=1)
-    packed = lax.all_gather(packed, "shard", axis=0, tiled=True)
+    packed = table_convert(packed)
     cuts = [width, width + kv_width, width + 2 * kv_width, 2 * width + 2 * kv_width]
     wq, wk, wv, wo, small = jnp.split(packed, cuts, axis=1)
     wr = small[:, :experts]

time: 844 us -> 890 us (1.055)
  waiting for transfers between devices: 285 us -> 326 us
  local copies, waits for them, and re-layouts: 73.7 us -> 82.9 us
    ppermute x0 -> x7, waiting for transfers between devices: none -> 85.2 us  [start_results(): w_next = lax.ppermute(tmp[0], along_axis, cards)]
    all_gather x1 -> x0, waiting for transfers between devices: 45.2 us -> none  [body(): packed = lax.all_gather(packed, 'shard', axis=0, tiled=True)]
    unnamed x142 -> x179, local copies, waits for them, and re-layouts: 8.41 us -> 18.8 us
  transfers between devices with their start and end apart: 6 -> 12, of which waited for: 4 -> 10; matrix products, arithmetic and copies ran while one was open for 31% -> 30% of each run, Pallas kernels for 0% -> 0%
where the time goes in v1:
time: 890 us; the launch traced here: 882 us
  matrix products  411 us (46%)
  waiting for transfers between devices  326 us (37%)
  local copies, waits for them, and re-layouts  82.9 us (9%)
  other arithmetic  44.1 us (5%)
  between operations  16.2 us (2%)
    all_gather x1, waiting for transfers between devices, body(): arrived = lax.all_gather(sent, axes, axis=0, tiled=True)  125 us
    all_gather x1, waiting for transfers between devices, body(): all_cot = lax.all_gather(cotangent, axes, axis=0, tiled=True)  88 us
    ppermute x7, waiting for transfers between devices, start_results(): w_next = lax.ppermute(tmp[0], along_axis, cards)  85.2 us
    dot_general x4, matrix products, gathered(): jnp.einsum('lmd,lmf->ldf', xg, d_gate, preferred_element_type=f32)  65.9 us
    dot_general x4, matrix products, gathered(): jnp.einsum('lmd,lmf->ldf', xg, d_up, preferred_element_type=f32)  58.8 us
    dot_general x4, matrix products, gathered(): jnp.einsum('lmf,lmd->lfd', scaled, cg, preferred_element_type=f32)  55.7 us
    dot_general x4, matrix products, gathered(): raw = jnp.einsum('lmd,lfd->lmf', cg, w_down, preferred_element_type=f32)  39.8 us
    dot_general x4, matrix products, gathered(): up_part = jnp.einsum('lmd,ldf->lmf', xg, w_up, preferred_element_type=f32)  38.3 us
  transfers between devices with their start and end apart: 12, of which 10 were waited for; matrix products, arithmetic and copies ran while one was open for 30% of the time, Pallas kernels for 0%

profile of v1, /device:TPU:0, one launch (start us, length us, event | category | flops | bytes accessed | tf_op | source)
XLA Modules:
  0.0 881.5 jit_solution(5889228728113937763)
XLA Ops:
  12.4 12.9 %collective-permute-done = bf16[128,3200]{1,0:T(8,128)(2,1)S(1)} collective-permute-done((bf16[128,3200]{1,0:T(8,128)(2,1)S(1)}, bf16[128,3200]{1,0:T(8,128)(2,1)S(1)}, u32[]{:S(2)}, u32[]{:S(2)}) %collective-permute-start) | collective-permute-done | bytes 819232 | tf_op jit(solution)/shard_map/ppermute | solution.py:31
  25.3 12.7 %collective-permute-done.1 = bf16[128,3200]{1,0:T(8,128)(2,1)S(1)} collective-permute-done((bf16[128,3200]{1,0:T(8,128)(2,1)S(1)}, bf16[128,3200]{1,0:T(8,128)(2,1)S(1)}, u32[]{:S(2)}, u32[]{:S(2)}) %collective-permute-start.1) | collective-permute-done | bytes 819232 | tf_op jit(solution)/shard_map/ppermute | solution.py:31
  38.0 12.7 %collective-permute-done.2 = bf16[128,3200]{1,0:T(8,128)(2,1)S(1)} collective-permute-done((bf16[128,3200]{1,0:T(8,128)(2,1)S(1)}, bf16[128,3200]{1,0:T(8,128)(2,1)S(1)}, u32[]{:S(2)}, u32[]{:S(2)}) %collective-permute-start.2) | collective-permute-done | bytes 819232 | tf_op jit(solution)/shard_map/ppermute | solution.py:31
  50.7 12.7 %collective-permute-done.3 = bf16[128,3200]{1,0:T(8,128)(2,1)S(1)} collective-permute-done((bf16[128,3200]{1,0:T(8,128)(2,1)S(1)}, bf16[128,3200]{1,0:T(8,128)(2,1)S(1)}, u32[]{:S(2)}, u32[]{:S(2)}) %collective-permute-start.3) | collective-permute-done | bytes 819232 | tf_op jit(solution)/shard_map/ppermute | solution.py:31
  64.2 12.8 %collective-permute-done.4 = bf16[128,3200]{1,0:T(8,128)(2,1)} collective-permute-done((bf16[128,3200]{1,0:T(8,128)(2,1)S(1)}, bf16[128,3200]{1,0:T(8,128)(2,1)}, u32[]{:S(2)}, u32[]{:S(2)}) %collective-permute-start.4) | collective-permute-done | bytes 819232 | tf_op jit(solution)/shard_map/ppermute | solution.py:31
  78.6 11.4 %collective-permute-done.5 = bf16[128,3200]{1,0:T(8,128)(2,1)} collective-permute-done((bf16[128,3200]{1,0:T(8,128)(2,1)}, bf16[128,3200]{1,0:T(8,128)(2,1)}, u32[]{:S(2)}, u32[]{:S(2)}) %collective-permute-start.5) | collective-permute-done | bytes 819232 | tf_op jit(solution)/shard_map/ppermute | solution.py:31
  92.7 10.2 %collective-permute-done.6 = bf16[128,3200]{1,0:T(8,128)(2,1)S(1)} collective-permute-done((bf16[128,3200]{1,0:T(8,128)(2,1)}, bf16[128,3200]{1,0:T(8,128)(2,1)S(1)}, u32[]{:S(2)}, u32[]{:S(2)}) %collective-permute-start.6) | collective-permute-done | bytes 819232 | tf_op jit(solution)/shard_map/ppermute | solution.py:31
  132.7 124.9 %all-gather.3.cloned.1.call-done = bf16[8192,1152]{1,0:T(8,128)(2,1)} async-done(((bf16[256,1152]{1,0:T(8,128)(2,1)}), bf16[8192,1152]{1,0:T(8,128)(2,1)}) %all-gather.3.cloned.1.call-update) | async-done | bytes 18874384 | tf_op jit(solution)/shard_map/all_gather | solution.py:162
  267.4 12.8 %dynamic-slice_bitcast_fusion = (bf16[8,256,1152]{2,1,0:T(8,128)(2,1)}, bf16[8,256,1152]{2,1,0:T(8,128)(2,1)S(1)}, bf16[8,256,1152]{2,1,0:T(8,128)(2,1)}, bf16[8,256,1152]{2,1,0:T(8,128)(2,1)}) fusion(bf16[4,8,256,1152]{3,2,1,0:T(8,128)(2,1)} %bitcast.302, s32[]{:T(128)S(6)} %select_n.101, s32[]{:T(128)S(6)} %select_n.98, s32[]{:T(128)S(6)} %select_n.95, ...), kind=kLoop, calls=%fused_computation.37 | loop fusion | bytes 37748752 | tf_op jit(solution)/shard_map/jit(dynamic_index_in_dim)/squeeze | solution.py:169
  285.5 88.0 %all-gather.5.cloned.1.call-done = bf16[8192,1024]{1,0:T(8,128)(2,1)} async-done(((bf16[256,1024]{1,0:T(8,128)(2,1)}), bf16[8192,1024]{1,0:T(8,128)(2,1)}) %all-gather.5.cloned.1.call-update) | async-done | bytes 16777232 | tf_op jit(solution)/shard_map/all_gather | solution.py:133
  401.0 8.7 fusion.241
  409.8 8.4 fusion.243
  418.1 10.2 %fusion.240 = f32[4,768,512]{1,2,0:T(8,128)} fusion(bf16[4,768,1024]{2,1,0:T(8,128)(2,1)} %bitcast.320, bf16[4,1024,512]{2,1,0:T(8,128)(2,1)} %param.26), kind=kOutput, calls=%fused_computation.321 | convolution fusion | flops 3221225472 | bytes 16777216 | tf_op jit(solution)/shard_map/lmd,ldf->lmf/dot_general | solution.py:179
  443.8 10.9 %fusion.232 = f32[4,768,512]{1,2,0:T(8,128)} fusion(bf16[4,768,1024]{2,1,0:T(8,128)(2,1)S(1)} %bitcast.295, bf16[4,1024,512]{2,1,0:T(8,128)(2,1)} %param.26), kind=kOutput, calls=%fused_computation.313 | convolution fusion | flops 3221225472 | bytes 16777216 | tf_op jit(solution)/shard_map/lmd,ldf->lmf/dot_general | solution.py:179
  486.3 15.0 %multiply_reduce_fusion = (f32[4,768]{1,0:T(4,128)S(1)}, f32[4,768,512]{1,2,0:T(8,128)}) fusion(f32[4,768,512]{1,2,0:T(8,128)} %fusion.232, f32[4,768,512]{1,2,0:T(8,128)} %fusion.231, bf16[4,768,1024]{2,1,0:T(8,128)(2,1)S(1)} %bitcast.299, bf16[4,512,1024]{2,1,0:T(8,128)(2,1)} %param.27), kind=kOutput, calls=%fused_computation.31 | convolution fusion | flops 3232232448 | bytes 29372416 | tf_op jit(solution)/shard_map/lmd,lfd->lmf/dot_general | solution.py:180
  504.6 8.4 multiply_convert_fusion.11
  532.9 9.6 %add_convert_fusion = bf16[4,768,1024]{2,1,0:T(8,128)(2,1)} fusion(f32[4,768,1024]{2,1,0:T(8,128)} %fusion.233, bf16[4,768,512]{1,2,0:T(8,128)(2,1)S(1)} %get-tuple-element.91, bf16[4,1024,512]{2,1,0:T(8,128)(2,1)} %param.26), kind=kOutput, calls=%fused_computation.4 | convolution fusion | flops 3227516928 | bytes 26214400 | tf_op jit(solution)/shard_map/lmf,ldf->lmd/dot_general | solution.py:198
  574.5 8.8 %fusion.237 = f32[4,768,512]{1,2,0:T(8,128)} fusion(bf16[4,768,1024]{2,1,0:T(8,128)(2,1)S(1)} %bitcast.328, bf16[4,1024,512]{2,1,0:T(8,128)(2,1)} %param.26), kind=kOutput, calls=%fused_computation.318 | convolution fusion | flops 3221225472 | bytes 16777216 | tf_op jit(solution)/shard_map/lmd,ldf->lmf/dot_general | solution.py:179
  583.3 11.0 %fusion.236 = f32[4,768,512]{1,2,0:T(8,128)} fusion(bf16[4,768,1024]{2,1,0:T(8,128)(2,1)} %bitcast.329, bf16[4,512,1024]{2,1,0:T(8,128)(2,1)} %param.27), kind=kOutput, calls=%fused_computation.317 | convolution fusion | flops 3221225472 | bytes 16777216 | tf_op jit(solution)/shard_map/lmd,lfd->lmf/dot_general | solution.py:180
  608.2 11.9 %fusion.39 = f32[4,512,1024]{2,1,0:T(8,128)} fusion(bf16[4,768,1024]{2,1,0:T(8,128)(2,1)S(1)} %bitcast.334, f32[4,768,512]{1,2,0:T(8,128)} %fusion.243, f32[4,768]{1,0:T(4,128)S(1)} %mul.784, f32[4,768,512]{1,2,0:T(8,128)} %fusion.244), kind=kOutput, calls=%fused_computation.79 | convolution fusion | flops 3232235520 | bytes 27275264 | tf_op jit(solution)/shard_map/lmf,lmd->lfd/dot_general | solution.py:191
  620.1 13.3 %fusion.38 = f32[4,512,1024]{2,1,0:T(8,128)} fusion(bf16[4,768,1024]{2,1,0:T(8,128)(2,1)} %bitcast.336, f32[4,768,512]{1,2,0:T(8,128)} %fusion.240, f32[4,768]{1,0:T(4,128)S(1)} %copy-done.51, f32[4,768,512]{1,2,0:T(8,128)} %fusion.241), kind=kOutput, calls=%fused_computation.78 | convolution fusion | flops 3232235520 | bytes 27275264 | tf_op jit(solution)/shard_map/lmf,lmd->lfd/dot_general | solution.py:191
  633.4 14.4 %fusion.35 = f32[4,1024,512]{2,1,0:T(8,128)} fusion(bf16[4,768,1024]{2,1,0:T(8,128)(2,1)} %bitcast.321, f32[4,768,512]{1,2,0:T(8,128)} %fusion.239, f32[4,768]{1,0:T(4,128)S(1)} %copy-done.51, f32[4,768,512]{1,2,0:T(8,128)} %fusion.241), kind=kOutput, calls=%fused_computation.75 | convolution fusion | flops 3232235520 | bytes 27275264 | tf_op jit(solution)/shard_map/lmd,lmf->ldf/dot_general | solution.py:190
  647.8 14.7 %fusion.36 = f32[4,1024,512]{2,1,0:T(8,128)} fusion(bf16[4,768,1024]{2,1,0:T(8,128)(2,1)} %bitcast.309, f32[4,768,512]{1,2,0:T(8,128)} %fusion.242, f32[4,768]{1,0:T(4,128)S(1)} %mul.784, f32[4,768,512]{1,2,0:T(8,128)} %fusion.244), kind=kOutput, calls=%fused_computation.76 | convolution fusion | flops 3232235520 | bytes 27275264 | tf_op jit(solution)/shard_map/lmd,lmf->ldf/dot_general | solution.py:190
  662.5 14.3 %fusion.34 = f32[4,1024,512]{2,1,0:T(8,128)} fusion(bf16[4,768,1024]{2,1,0:T(8,128)(2,1)} %bitcast.323, f32[4,768,512]{1,2,0:T(8,128)} %fusion.236, f32[4,768]{1,0:T(4,128)S(1)} %copy-done.49, f32[4,768,512]{1,2,0:T(8,128)} %fusion.238), kind=kOutput, calls=%fused_computation.74 | convolution fusion | flops 3232235520 | bytes 27275264 | tf_op jit(solution)/shard_map/lmd,lmf->ldf/dot_general | solution.py:190
  725.1 14.6 %fusion.37 = f32[4,512,1024]{2,1,0:T(8,128)} fusion(bf16[4,768,1024]{2,1,0:T(8,128)(2,1)} %bitcast.330, f32[4,768,512]{1,2,0:T(8,128)} %fusion.237, f32[4,768]{1,0:T(4,128)S(1)} %copy-done.50, f32[4,768,512]{1,2,0:T(8,128)} %fusion.238), kind=kOutput, calls=%fused_computation.77 | convolution fusion | flops 3232235520 | bytes 27275264 | tf_op jit(solution)/shard_map/lmf,lmd->lfd/dot_general | solution.py:191
  739.7 9.7 %fusion.235 = f32[4,1024,512]{2,1,0:T(8,128)} fusion(bf16[4,768,1024]{2,1,0:T(8,128)(2,1)} %bitcast.297, bf16[4,768,512]{1,2,0:T(8,128)(2,1)S(1)} %copy-done.6), kind=kOutput, calls=%fused_computation.316 | convolution fusion | flops 3221225472 | bytes 17825792 | tf_op jit(solution)/shard_map/lmd,lmf->ldf/dot_general | solution.py:189
  749.5 17.3 %fusion.47 = f32[4,1024,512]{2,1,0:T(8,128)} fusion(bf16[4,768,1024]{2,1,0:T(8,128)(2,1)} %bitcast.322, f32[4,768,512]{1,2,0:T(8,128)} %fusion.241, f32[4,768,512]{1,2,0:T(8,128)} %fusion.240, f32[4,768,512]{1,2,0:T(8,128)} %fusion.239, f32[4,768]{1,0:T(4,128)S(1)} %copy-done.52), kind=kOutput, calls=%fused_computation.96 | convolution fusion | flops 3238526976 | bytes 33566720 | tf_op jit(solution)/shard_map/lmd,lmf->ldf/dot_general | solution.py:189
  766.8 17.1 %fusion.46 = f32[4,1024,512]{2,1,0:T(8,128)} fusion(bf16[4,768,1024]{2,1,0:T(8,128)(2,1)} %bitcast.324, f32[4,768,512]{1,2,0:T(8,128)} %fusion.238, f32[4,768,512]{1,2,0:T(8,128)} %fusion.237, f32[4,768,512]{1,2,0:T(8,128)} %fusion.236, f32[4,768]{1,0:T(4,128)S(1)} %copy-done.50), kind=kOutput, calls=%fused_computation.95 | convolution fusion | flops 3238526976 | bytes 33566720 | tf_op jit(solution)/shard_map/lmd,lmf->ldf/dot_general | solution.py:189
  783.9 15.8 %add_add_fusion = f32[4,512,1024]{2,1,0:T(8,128)} fusion(f32[4,512,1024]{2,1,0:T(8,128)} %fusion.39, f32[4,512,1024]{2,1,0:T(8,128)} %fusion.38, f32[4,512,1024]{2,1,0:T(8,128)} %fusion.37, bf16[4,768,512]{1,2,0:T(8,128)(2,1)S(1)} %copy-done.8, bf16[4,768,1024]{2,1,0:T(8,128)(2,1)} %bitcast.300), kind=kOutput, calls=%fused_computation.8 | convolution fusion | flops 3227516928 | bytes 42991616 | tf_op jit(solution)/shard_map/lmf,lmd->lfd/dot_general | solution.py:191
  799.7 21.8 %add_add_fusion.2 = f32[4,1024,512]{2,1,0:T(8,128)} fusion(f32[4,1024,512]{2,1,0:T(8,128)} %fusion.47, f32[4,1024,512]{2,1,0:T(8,128)} %fusion.235, f32[4,1024,512]{2,1,0:T(8,128)} %fusion.46, bf16[4,768,1024]{2,1,0:T(8,128)(2,1)} %bitcast.310, f32[4,768,512]{1,2,0:T(8,128)} %fusion.244, f32[4,768,512]{1,2,0:T(8,128)} %fusion.243, ...), kind=kOutput, calls=%fused_computation.10 | convolution fusion | flops 3244818432 | bytes 58732544 | tf_op jit(solution)/shard_map/lmd,lmf->ldf/dot_general | solution.py:189
  821.5 15.4 %add_add_fusion.1 = f32[4,1024,512]{2,1,0:T(8,128)} fusion(f32[4,1024,512]{2,1,0:T(8,128)} %fusion.36, f32[4,1024,512]{2,1,0:T(8,128)} %fusion.35, f32[4,1024,512]{2,1,0:T(8,128)} %fusion.34, bf16[4,768,1024]{2,1,0:T(8,128)(2,1)} %bitcast.298, bf16[4,768,512]{1,2,0:T(8,128)(2,1)S(1)} %copy-done.3), kind=kOutput, calls=%fused_computation.9 | convolution fusion | flops 3227516928 | bytes 42991616 | tf_op jit(solution)/shard_map/lmd,lmf->ldf/dot_general | solution.py:190
  840.0 27.3 %all-reduce.4.cloned.1.call-done = bf16[128,3200]{1,0:T(8,128)(2,1)} async-done(((bf16[128,3200]{1,0:T(8,128)(2,1)}), bf16[128,3200]{1,0:T(8,128)(2,1)}) %all-reduce.4.cloned.1.call-update) | async-done | bytes 819216 | tf_op jit(solution)/shard_map/psum | solution.py:255
  (340 shorter events, 255.7 us)
Async XLA Ops:
  7.2 250.4 %all-gather.3.cloned.1.call-start = ((), (), s32[]{:S(2)}) async-start(), calls=%async_computation.2 | async-start | bytes 19464192 | tf_op jit(solution)/shard_map/all_gather | solution.py:162
  11.9 95.2 %copy-start.22 = (bf16[128,1024]{1,0:T(8,128)(2,1)S(1)}, bf16[128,1024]{1,0:T(8,128)(2,1)}, u32[]{:S(2)}) copy-start(bf16[128,1024]{1,0:T(8,128)(2,1)} %param.18) | copy-start | bytes 786436
  11.9 13.4 %collective-permute-start = (bf16[128,3200]{1,0:T(8,128)(2,1)S(1)}, bf16[128,3200]{1,0:T(8,128)(2,1)S(1)}, u32[]{:S(2)}, u32[]{:S(2)}) collective-permute-start(bf16[128,3200]{1,0:T(8,128)(2,1)S(1)} %constant_dynamic-update-slice_fusion), channel_id=1, source_target_pairs={{0,1},{1,2},{2,3},{3,4},{4,5},{5,6},{6,7},{7,0},{8,9},{9,10},{10,1... | collective-permute-start | bytes 2457608 | tf_op jit(solution)/shard_map/ppermute | solution.py:31
  25.3 12.7 %collective-permute-start.1 = (bf16[128,3200]{1,0:T(8,128)(2,1)S(1)}, bf16[128,3200]{1,0:T(8,128)(2,1)S(1)}, u32[]{:S(2)}, u32[]{:S(2)}) collective-permute-start(bf16[128,3200]{1,0:T(8,128)(2,1)S(1)} %collective-permute-done), channel_id=1, source_target_pairs={{0,1},{1,2},{2,3},{3,4},{4,5},{5,6},{6,7},{7,0},{8,9},{9,10},{10,1... | collective-permute-start | bytes 2457608 | tf_op jit(solution)/shard_map/ppermute | solution.py:31
  38.0 12.7 %collective-permute-start.2 = (bf16[128,3200]{1,0:T(8,128)(2,1)S(1)}, bf16[128,3200]{1,0:T(8,128)(2,1)S(1)}, u32[]{:S(2)}, u32[]{:S(2)}) collective-permute-start(bf16[128,3200]{1,0:T(8,128)(2,1)S(1)} %collective-permute-done.1), channel_id=1, source_target_pairs={{0,1},{1,2},{2,3},{3,4},{4,5},{5,6},{6,7},{7,0},{8,9},{9,10},{10,1... | collective-permute-start | bytes 2457608 | tf_op jit(solution)/shard_map/ppermute | solution.py:31
  50.7 12.7 %collective-permute-start.3 = (bf16[128,3200]{1,0:T(8,128)(2,1)S(1)}, bf16[128,3200]{1,0:T(8,128)(2,1)S(1)}, u32[]{:S(2)}, u32[]{:S(2)}) collective-permute-start(bf16[128,3200]{1,0:T(8,128)(2,1)S(1)} %collective-permute-done.2), channel_id=1, source_target_pairs={{0,1},{1,2},{2,3},{3,4},{4,5},{5,6},{6,7},{7,0},{8,9},{9,10},{10,1... | collective-permute-start | bytes 2457608 | tf_op jit(solution)/shard_map/ppermute | solution.py:31
  64.2 12.8 %collective-permute-start.4 = (bf16[128,3200]{1,0:T(8,128)(2,1)S(1)}, bf16[128,3200]{1,0:T(8,128)(2,1)}, u32[]{:S(2)}, u32[]{:S(2)}) collective-permute-start(bf16[128,3200]{1,0:T(8,128)(2,1)S(1)} %collective-permute-done.3), channel_id=1, source_target_pairs={{0,1},{1,2},{2,3},{3,4},{4,5},{5,6},{6,7},{7,0},{8,9},{9,10},{10,1... | collective-permute-start | bytes 2457608 | tf_op jit(solution)/shard_map/ppermute | solution.py:31
  77.0 13.0 %collective-permute-start.5 = (bf16[128,3200]{1,0:T(8,128)(2,1)}, bf16[128,3200]{1,0:T(8,128)(2,1)}, u32[]{:S(2)}, u32[]{:S(2)}) collective-permute-start(bf16[128,3200]{1,0:T(8,128)(2,1)} %collective-permute-done.4), channel_id=1, source_target_pairs={{0,1},{1,2},{2,3},{3,4},{4,5},{5,6},{6,7},{7,0},{8,9},{9,10},{10,1... | collective-permute-start | bytes 2457608 | tf_op jit(solution)/shard_map/ppermute | solution.py:31
  78.5 28.5 %copy-start.26 = (bf16[128,512]{1,0:T(8,128)(2,1)S(1)}, bf16[128,512]{1,0:T(8,128)(2,1)}, u32[]{:S(2)}) copy-start(bf16[128,512]{1,0:T(8,128)(2,1)} %param.19) | copy-start | bytes 393220
  90.0 12.9 %collective-permute-start.6 = (bf16[128,3200]{1,0:T(8,128)(2,1)}, bf16[128,3200]{1,0:T(8,128)(2,1)S(1)}, u32[]{:S(2)}, u32[]{:S(2)}) collective-permute-start(bf16[128,3200]{1,0:T(8,128)(2,1)} %collective-permute-done.5), channel_id=1, source_target_pairs={{0,1},{1,2},{2,3},{3,4},{4,5},{5,6},{6,7},{7,0},{8,9},{9,10},{10,1... | collective-permute-start | bytes 2457608 | tf_op jit(solution)/shard_map/ppermute | solution.py:31
  91.2 15.9 %copy-start.27 = (bf16[128,512]{1,0:T(8,128)(2,1)S(1)}, bf16[128,512]{1,0:T(8,128)(2,1)}, u32[]{:S(2)}) copy-start(bf16[128,512]{1,0:T(8,128)(2,1)} %param.20) | copy-start | bytes 393220
  91.8 24.0 %copy-start.53 = (f32[256]{0:T(256)}, f32[256]{0:T(256)S(1)}, u32[]{:S(2)}) copy-start(f32[256]{0:T(256)S(1)} %get-tuple-element.111) | copy-start | bytes 3076
  91.9 15.3 %copy-start.23 = (bf16[128,1024]{1,0:T(8,128)(2,1)S(1)}, bf16[128,1024]{1,0:T(8,128)(2,1)}, u32[]{:S(2)}) copy-start(bf16[128,1024]{1,0:T(8,128)(2,1)} %param.21) | copy-start | bytes 786436
  92.7 25.1 %copy-start.31 = (f32[256,32]{0,1:T(8,128)}, f32[256,32]{0,1:T(8,128)S(1)}, u32[]{:S(2)}) copy-start(f32[256,32]{0,1:T(8,128)S(1)} %get-tuple-element.116) | copy-start | bytes 98308
  110.8 16.8 %copy-start.43 = (f32[1024]{0:T(1024)}, f32[1024]{0:T(1024)S(1)}, u32[]{:S(2)}) copy-start(f32[1024]{0:T(1024)S(1)} %get-tuple-element.72) | copy-start | bytes 12292
  127.6 133.1 %copy-start.47 = (f32[256]{0:T(256)}, f32[256]{0:T(256)S(1)}, u32[]{:S(2)}) copy-start(f32[256]{0:T(256)S(1)} %get-tuple-element.113) | copy-start | bytes 3076
  128.1 135.1 %copy-start.15 = (bf16[256,1024]{1,0:T(8,128)(2,1)}, bf16[256,1024]{1,0:T(8,128)(2,1)S(1)}, u32[]{:S(2)}) copy-start(bf16[256,1024]{1,0:T(8,128)(2,1)S(1)} %multiply_convert_fusion.24) | copy-start | bytes 1572868
  131.7 241.8 %all-gather.5.cloned.1.call-start = ((), (), s32[]{:S(2)}) async-start(), calls=%async_computation.3 | async-start | bytes 17301504 | tf_op jit(solution)/shard_map/all_gather | solution.py:133
  132.5 544.4 %reduce-scatter.3.cloned.1.call-start = ((), (), s32[]{:S(2)}) async-start(), calls=%async_computation.4 | async-start | bytes 10027008 | tf_op jit(solution)/shard_map/reduce_scatter | solution.py:216
  513.1 19.8 %copy-start.2 = (bf16[4,768,512]{1,2,0:T(8,128)(2,1)}, bf16[4,768,512]{1,2,0:T(8,128)(2,1)S(1)}, u32[]{:S(2)}) copy-start(bf16[4,768,512]{1,2,0:T(8,128)(2,1)S(1)} %get-tuple-element.91) | copy-start | bytes 9437188
  558.8 262.7 %reduce-scatter.5.cloned.1.call-start = ((), (), s32[]{:S(2)}) async-start(), calls=%async_computation.5 | async-start | bytes 7372800 | tf_op jit(solution)/shard_map/reduce_scatter | solution.py:254
  583.3 19.3 %slice-start.6 = ((s8[6291456]{0:T(1024)(128)(4,1)}), s8[4194304]{0:T(1024)(128)(4,1)S(1)}, s32[]{:S(2)}) async-start(s8[6291456]{0:T(1024)(128)(4,1)} %bitcast.331), calls=%async_computation.13 | async-start | bytes 8388608
  662.5 15.8 %copy-start.28 = (f32[256,32]{1,0:T(8,128)S(1)}, f32[256,32]{1,0:T(8,128)}, u32[]{:S(2)}) copy-start(f32[256,32]{1,0:T(8,128)} %get-tuple-element.84) | copy-start | bytes 98308
  662.5 16.0 %copy-start.16 = (bf16[256,1024]{1,0:T(8,128)(2,1)S(1)}, bf16[256,1024]{1,0:T(8,128)(2,1)}, u32[]{:S(2)}) copy-start(bf16[256,1024]{1,0:T(8,128)(2,1)} %copy-done.15) | copy-start | bytes 1572868
  662.5 16.3 %copy-start.14 = (f32[256,1024]{1,0:T(8,128)S(1)}, f32[256,1024]{1,0:T(8,128)}, u32[]{:S(2)}) copy-start(f32[256,1024]{1,0:T(8,128)} %copy-done.13) | copy-start | bytes 3145732
  662.5 16.3 %copy-start.44 = (f32[1024]{0:T(1024)S(1)}, f32[1024]{0:T(1024)}, u32[]{:S(2)}) copy-start(f32[1024]{0:T(1024)} %copy-done.43) | copy-start | bytes 12292
  662.5 16.3 %copy-start.48 = (f32[256]{0:T(256)S(1)}, f32[256]{0:T(256)}, u32[]{:S(2)}) copy-start(f32[256]{0:T(256)} %copy-done.47) | copy-start | bytes 3076
  724.4 15.3 %copy-start.6 = (bf16[4,768,512]{1,2,0:T(8,128)(2,1)S(1)}, bf16[4,768,512]{1,2,0:T(8,128)(2,1)}, u32[]{:S(2)}) copy-start(bf16[4,768,512]{1,2,0:T(8,128)(2,1)} %copy-done.5) | copy-start | bytes 9437188
  724.4 142.8 %all-reduce.4.cloned.1.call-start = ((), (), s32[]{:S(2)}) async-start(), calls=%async_computation.6 | async-start | bytes 1638400 | tf_op jit(solution)/shard_map/psum | solution.py:255
  766.8 17.1 %copy-start.8 = (bf16[4,768,512]{1,2,0:T(8,128)(2,1)S(1)}, bf16[4,768,512]{1,2,0:T(8,128)(2,1)}, u32[]{:S(2)}) copy-start(bf16[4,768,512]{1,2,0:T(8,128)(2,1)} %copy-done.7) | copy-start | bytes 9437188
  799.7 21.8 %copy-start.3 = (bf16[4,768,512]{1,2,0:T(8,128)(2,1)S(1)}, bf16[4,768,512]{1,2,0:T(8,128)(2,1)}, u32[]{:S(2)}) copy-start(bf16[4,768,512]{1,2,0:T(8,128)(2,1)} %copy-done.2) | copy-start | bytes 9437188
  821.5 15.4 %copy-start.56 = (f32[256]{0:T(256)S(1)}, f32[256]{0:T(256)}, u32[]{:S(2)}) copy-start(f32[256]{0:T(256)} %get-tuple-element.110) | copy-start | bytes 3076
  (55 other events, 384.0 us)
Sparse Core Ops, SparseCore 0:
  131.8 125.7 all-gather.2
  260.5 113.0 all-gather.4
  558.9 74.1 reduce-scatter.2
  724.5 63.5 reduce-scatter.4
  821.6 45.5 all-reduce.3
